TPU v7x, 32 devices: a whole 2x2x4 slice. The times are simulated.
32 devices in a mesh: ctx: 8 (over z, y), fsdp: 4 (over x, core).
Axes of the slice: x: 2, y: 2, z: 4, core: 2. Of those that a mesh axis runs over, the one named last changes fastest.
Arguments:
- tokens: bfloat16 [4, 1024, 768], P('fsdp', 'ctx'), may hold values from -6 to 6
- routes: int32 [4, 1024, 2], P('fsdp', 'ctx'), may hold values from 0 to 63, all different within a row; in each aligned block of 128 rows (0 to 127, 128 to 255, ..., all dimensions but the last counted through in order) at most 8 rows name the same one
- cotangent: bfloat16 [4, 1024, 768], P('fsdp', 'ctx'), may hold values from -6 to 6
- gains: bfloat16 [2, 768], P(None, ('ctx', 'fsdp')), may hold values from 0.25 to 1.75
- rel_bias: bfloat16 [384], P(('ctx', 'fsdp')), may hold values from -4 to 4
- attn_qkv: bfloat16 [2304, 768], P(('ctx', 'fsdp')), may hold values from -1.25 to 1.25
- attn_out: bfloat16 [768, 768], P(('ctx', 'fsdp')), may hold values from -0.875 to 0.875
- router: bfloat16 [768, 64], P(('ctx', 'fsdp')), may hold values from -0.875 to 0.875
- w_in: bfloat16 [64, 768, 3072], P('ctx', None, 'fsdp'), may hold values from -0.21875 to 0.21875
- w_out: bfloat16 [64, 3072, 768], P('ctx', 'fsdp'), may hold values from -0.109375 to 0.109375
Outputs:
- mixed: bfloat16 [4, 1024, 768], P('fsdp', 'ctx')
- d_tokens: float32 [4, 1024, 768], P('fsdp', 'ctx')
- d_gains: float32 [2, 768], P(None, ('ctx', 'fsdp'))
- d_rel_bias: float32 [384], P(('ctx', 'fsdp'))
- d_attn_qkv: float32 [2304, 768], P(('ctx', 'fsdp'))
- d_attn_out: float32 [768, 768], P(('ctx', 'fsdp'))
- d_router: float32 [768, 64], P(('ctx', 'fsdp'))
- d_w_in: float32 [64, 768, 3072], P('ctx', None, 'fsdp')
- d_w_out: float32 [64, 3072, 768], P('ctx', 'fsdp')
Inputs may be any that keep to these rules, and one draw needn't show every extreme that they name: The two routes of a token name different experts. In each aligned block of 128 tokens of a sequence no expert is named more than 8 times, and some block names some expert exactly 8 times.
All inputs are finite; a program needn't handle non-finite values.
Results may differ from a plain program's by a relative error of at most 0.017.
The roundings to bfloat16 on the way count: a program that leaves them out, or rounds other values in their place, can miss the bound.
Values may be sent and summed in bfloat16 or wider, within the bound.
A program may use at most 320 MiB of HBM per device.

v0:
```python
import math

import jax
import jax.numpy as jnp
from jax import lax
from jax.sharding import PartitionSpec as P

D = 768
H = 12
DH = 64
E = 64
NB = 32
CAP = 8


EPS = 1e-06
EDGES = (16, 23, 32, 45, 64, 91, 128, 181, 256, 362, 512, 724, 1024, 1448, 2048, 2896)
GELU_C = 0.7978845608028654
NEG = -1e30


def bucket_of(offset):
    clipped = jnp.maximum(offset, 0)
    far = 15 + sum(((clipped >= edge).astype(jnp.int32) for edge in EDGES))
    return jnp.where(clipped < 16, clipped, far)


def norm_forward(values):
    inverse_norm = lax.rsqrt(jnp.mean(values * values, axis=-1, keepdims=True) + EPS)
    return (values * inverse_norm, inverse_norm)


def norm_backward(normalized_gradient, centered_rows, inverse_norm, gain_vector):
    centered_gradient = normalized_gradient * gain_vector
    gain_gradient = jnp.sum(normalized_gradient * centered_rows, axis=0)
    value_gradients = inverse_norm * (
        centered_gradient
        - centered_rows * jnp.mean(centered_gradient * centered_rows, axis=-1, keepdims=True)
    )
    return (value_gradients, gain_gradient)


def gelu_parts(pre):
    inner = GELU_C * (pre + 0.044715 * pre * pre * pre)
    tanh_v = jnp.tanh(inner)
    value = 0.5 * pre * (1.0 + tanh_v)
    slope = 0.5 * (1.0 + tanh_v) + 0.5 * pre * (1.0 - tanh_v * tanh_v) * GELU_C * (
        1.0 + 3.0 * 0.044715 * pre * pre
    )
    return (value, slope)


def block_terms(qheads, kpart, bias_table, qstart, kstart, scale):
    score = jnp.einsum("qhd,khd->hqk", qheads, kpart, preferred_element_type=jnp.float32) * scale
    offset = (qstart + jnp.arange(qheads.shape[0], dtype=jnp.int32))[:, None] - (
        kstart + jnp.arange(kpart.shape[0], dtype=jnp.int32)
    )[None, :]
    one_hot_mask = (
        bucket_of(offset)[None] == jnp.arange(NB, dtype=jnp.int32)[:, None, None]
    ).astype(jnp.bfloat16)
    bias_term = jnp.einsum(
        "fz,zmp->fmp", bias_table, one_hot_mask, preferred_element_type=jnp.float32
    )
    return (jnp.where(offset[None] >= 0, score + bias_term, -jnp.inf), one_hot_mask)


def shards(tokens, routes, cotangent, gains, rel_bias, attn_qkv, attn_out, router, w_in, w_out):
    single_float = jnp.float32
    bfloat_half = jnp.bfloat16
    tok = tokens.shape[1]
    n_ctx = lax.axis_size("ctx")
    seq_len = tok * n_ctx
    qstart = lax.axis_index("ctx") * tok
    qlast = qstart + tok - 1
    per_dev = w_in.shape[0]
    scale = 1.0 / math.sqrt(DH)
    kblk = math.gcd(seq_len, 512)
    qkv_full, out_full, router_full, gains_full, bias_full = (
        lax.all_gather(attn_qkv, ("ctx", "fsdp"), axis=0, tiled=True),
        lax.all_gather(attn_out, ("ctx", "fsdp"), axis=0, tiled=True),
        lax.all_gather(router, ("ctx", "fsdp"), axis=0, tiled=True),
        lax.all_gather(gains, ("ctx", "fsdp"), axis=1, tiled=True),
        lax.all_gather(rel_bias, ("ctx", "fsdp"), axis=0, tiled=True),
    )
    w_qkv = qkv_full.reshape(3, D, D)
    bias_table = bias_full.reshape(H, NB)
    first_gain = gains_full[0].astype(single_float)
    second_gain = gains_full[1].astype(single_float)
    input_rows = tokens.reshape(tok, D).astype(single_float)
    first_centered, first_inverse_norm = norm_forward(input_rows)
    first_normalized = (first_centered * first_gain).astype(bfloat_half)
    q = jnp.dot(first_normalized, w_qkv[0], preferred_element_type=single_float).astype(bfloat_half)
    k = jnp.dot(first_normalized, w_qkv[1], preferred_element_type=single_float).astype(bfloat_half)
    v = jnp.dot(first_normalized, w_qkv[2], preferred_element_type=single_float).astype(bfloat_half)
    keys_all, values_all = (
        lax.all_gather(k, "ctx", axis=0, tiled=True),
        lax.all_gather(v, "ctx", axis=0, tiled=True),
    )
    qheads = q.reshape(tok, H, DH)
    kheads = keys_all.reshape(seq_len, H, DH)
    vheads = values_all.reshape(seq_len, H, DH)

    def keep(carry):
        return carry

    def forward_step(index, carry):
        kstart = index * kblk

        def forward_live(state):
            run_max, total, acc = state
            kpart = lax.dynamic_slice_in_dim(kheads, kstart, kblk, 0)
            vpart = lax.dynamic_slice_in_dim(vheads, kstart, kblk, 0)
            score, _ = block_terms(qheads, kpart, bias_table, qstart, kstart, scale)
            newest = jnp.maximum(run_max, jnp.max(score, axis=-1))
            factor = jnp.exp(run_max - newest)
            weights = jnp.exp(score - newest[..., None])
            total = total * factor + jnp.sum(weights, axis=-1)
            acc = acc * factor[..., None] + jnp.einsum(
                "hqk,khd->hqd",
                weights.astype(bfloat_half),
                vpart,
                preferred_element_type=single_float,
            )
            return (newest, total, acc)

        return lax.cond(kstart <= qlast, forward_live, keep, carry)

    init = (
        jnp.full((H, tok), NEG, single_float),
        jnp.zeros((H, tok), single_float),
        jnp.zeros((H, tok, DH), single_float),
    )
    run_max, total, acc = lax.fori_loop(0, seq_len // kblk, forward_step, init)
    lse = run_max + jnp.log(total)
    attended = (acc / total[..., None]).transpose(1, 0, 2).reshape(tok, D).astype(bfloat_half)
    first_hidden = input_rows + jnp.dot(attended, out_full, preferred_element_type=single_float)
    second_centered, second_inverse_norm = norm_forward(first_hidden)
    second_normalized = (second_centered * second_gain).astype(bfloat_half)
    logits = jnp.dot(second_normalized, router_full, preferred_element_type=single_float)
    expert_ids = jnp.arange(E, dtype=jnp.int32)
    chosen_mask = (routes.reshape(tok, 2)[:, :, None] == expert_ids).astype(single_float)
    chosen = jnp.sum(logits[:, None, :] * chosen_mask, axis=-1)
    gate = jax.nn.softmax(chosen, axis=-1)
    flat_routes = routes.reshape(2 * tok)
    member = (flat_routes[:, None] == expert_ids[None, :]).astype(jnp.int32)
    slot = jnp.sum((jnp.cumsum(member, axis=0) - member) * member, axis=1)
    target = flat_routes * CAP + slot
    table_disp = (target[:, None] == jnp.arange(E * CAP, dtype=jnp.int32)[None, :]).astype(
        bfloat_half
    )
    doubled = jnp.repeat(second_normalized, 2, axis=0)
    packed = (
        jnp.einsum("ac,ad->cd", table_disp, doubled, preferred_element_type=single_float)
        .astype(bfloat_half)
        .reshape(n_ctx, per_dev, CAP, D)
    )
    received = lax.all_to_all(packed, "ctx", split_axis=0, concat_axis=0, tiled=True)
    w_in_full, w_out_full = (
        lax.all_gather(w_in, "fsdp", axis=2, tiled=True),
        lax.all_gather(w_out, "fsdp", axis=1, tiled=True),
    )
    hid, slope = gelu_parts(
        jnp.einsum("sjcd,jdf->sjcf", received, w_in_full, preferred_element_type=single_float)
    )
    hid_bf = hid.astype(bfloat_half)
    expert_out = jnp.einsum(
        "sjcf,jfd->sjcd", hid_bf, w_out_full, preferred_element_type=single_float
    ).astype(bfloat_half)
    returned = lax.all_to_all(expert_out, "ctx", split_axis=0, concat_axis=0, tiled=True)
    picked = jnp.einsum(
        "ac,cd->ad", table_disp, returned.reshape(E * CAP, D), preferred_element_type=single_float
    ).reshape(tok, 2, D)
    mixed = (first_hidden + jnp.sum(gate[:, :, None] * picked, axis=1)).astype(bfloat_half)
    dy = cotangent.reshape(tok, D).astype(single_float)
    dgate = jnp.sum(dy[:, None, :] * picked, axis=-1)
    dchosen = gate * (dgate - jnp.sum(gate * dgate, axis=-1, keepdims=True))
    dlogits = jnp.sum(chosen_mask * dchosen[:, :, None], axis=1).astype(bfloat_half)
    dpicked = (gate[:, :, None] * dy[:, None, :]).astype(bfloat_half).reshape(2 * tok, D)
    dpacked = (
        jnp.einsum("ac,ad->cd", table_disp, dpicked, preferred_element_type=single_float)
        .astype(bfloat_half)
        .reshape(n_ctx, per_dev, CAP, D)
    )
    dreceived = lax.all_to_all(dpacked, "ctx", split_axis=0, concat_axis=0, tiled=True)
    dhid = jnp.einsum("sjcd,jfd->sjcf", dreceived, w_out_full, preferred_element_type=single_float)
    dpre = (dhid * slope).astype(bfloat_half)
    d_w_out_whole = jnp.einsum(
        "sjcf,sjcd->jfd", hid_bf, dreceived, preferred_element_type=single_float
    )
    d_w_in_whole = jnp.einsum("sjcd,sjcf->jdf", received, dpre, preferred_element_type=single_float)
    dreturn = jnp.einsum(
        "sjcf,jdf->sjcd", dpre, w_in_full, preferred_element_type=single_float
    ).astype(bfloat_half)
    d_w_in_mine, d_w_out_mine = (
        lax.psum_scatter(
            d_w_in_whole.astype(jnp.bfloat16), "fsdp", scatter_dimension=2, tiled=True
        ).astype(jnp.float32),
        lax.psum_scatter(
            d_w_out_whole.astype(jnp.bfloat16), "fsdp", scatter_dimension=1, tiled=True
        ).astype(jnp.float32),
    )
    dback = lax.all_to_all(dreturn, "ctx", split_axis=0, concat_axis=0, tiled=True).reshape(
        E * CAP, D
    )
    second_normalized_gradient = jnp.sum(
        jnp.einsum("ac,cd->ad", table_disp, dback, preferred_element_type=single_float).reshape(
            tok, 2, D
        ),
        axis=1,
    )
    second_normalized_gradient = second_normalized_gradient + jnp.einsum(
        "te,de->td", dlogits, router_full, preferred_element_type=single_float
    )
    d_router_part = jnp.einsum(
        "td,te->de", second_normalized, dlogits, preferred_element_type=single_float
    )
    second_norm_gradient, second_gain_gradient = norm_backward(
        second_normalized_gradient, second_centered, second_inverse_norm, second_gain
    )
    dh1 = dy + second_norm_gradient
    dh1_bf = dh1.astype(bfloat_half)
    d_out_part = jnp.einsum("td,te->de", attended, dh1_bf, preferred_element_type=single_float)
    dattended = jnp.einsum(
        "te,de->td", dh1_bf, out_full, preferred_element_type=single_float
    ).astype(bfloat_half)
    do_heads = dattended.reshape(tok, H, DH)
    delta = jnp.sum(
        (dattended.astype(single_float) * attended.astype(single_float)).reshape(tok, H, DH),
        axis=-1,
    ).T

    def backward_step(index, carry):
        kstart = index * kblk

        def backward_live(state):
            dq, dk_all, dv_all, dtable = state
            kpart = lax.dynamic_slice_in_dim(kheads, kstart, kblk, 0)
            vpart = lax.dynamic_slice_in_dim(vheads, kstart, kblk, 0)
            score, one_hot_mask = block_terms(qheads, kpart, bias_table, qstart, kstart, scale)
            weight = jnp.exp(score - lse[..., None])
            weight_bf = weight.astype(bfloat_half)
            dweight = jnp.einsum(
                "qhd,khd->hqk", do_heads, vpart, preferred_element_type=single_float
            )
            score_gradient = weight * (dweight - delta[..., None])
            dscore_bf = score_gradient.astype(bfloat_half)
            dtable = dtable + jnp.einsum(
                "vwi,rwi->vr",
                score_gradient,
                one_hot_mask.astype(single_float),
                precision=lax.Precision.HIGHEST,
            )
            dq = (
                dq
                + jnp.einsum("hqk,khd->qhd", dscore_bf, kpart, preferred_element_type=single_float)
                * scale
            )
            dk_piece = (
                jnp.einsum("hqk,qhd->khd", dscore_bf, qheads, preferred_element_type=single_float)
                * scale
            )
            dv_piece = jnp.einsum(
                "hqk,qhd->khd", weight_bf, do_heads, preferred_element_type=single_float
            )
            dk_all = lax.dynamic_update_slice_in_dim(dk_all, dk_piece, kstart, 0)
            dv_all = lax.dynamic_update_slice_in_dim(dv_all, dv_piece, kstart, 0)
            return (dq, dk_all, dv_all, dtable)

        return lax.cond(kstart <= qlast, backward_live, keep, carry)

    init_back = (
        jnp.zeros((tok, H, DH), single_float),
        jnp.zeros((seq_len, H, DH), single_float),
        jnp.zeros((seq_len, H, DH), single_float),
        jnp.zeros((H, NB), single_float),
    )
    dq, dk_all, dv_all, dtable = lax.fori_loop(0, seq_len // kblk, backward_step, init_back)
    dk_mine, dv_mine = (
        lax.psum_scatter(
            dk_all.reshape(seq_len, D).astype(jnp.bfloat16), "ctx", scatter_dimension=0, tiled=True
        ).astype(jnp.float32),
        lax.psum_scatter(
            dv_all.reshape(seq_len, D).astype(jnp.bfloat16), "ctx", scatter_dimension=0, tiled=True
        ).astype(jnp.float32),
    )
    grads_in = (
        dq.reshape(tok, D).astype(bfloat_half),
        dk_mine.astype(bfloat_half),
        dv_mine.astype(bfloat_half),
    )
    d_qkv_part = jnp.concatenate(
        [
            jnp.einsum("td,te->de", first_normalized, part, preferred_element_type=single_float)
            for part in grads_in
        ],
        axis=0,
    )
    first_normalized_gradient = jnp.einsum(
        "te,de->td", grads_in[0], w_qkv[0], preferred_element_type=single_float
    )
    first_normalized_gradient = first_normalized_gradient + jnp.einsum(
        "te,de->td", grads_in[1], w_qkv[1], preferred_element_type=single_float
    )
    first_normalized_gradient = first_normalized_gradient + jnp.einsum(
        "te,de->td", grads_in[2], w_qkv[2], preferred_element_type=single_float
    )
    first_norm_gradient, first_gain_gradient = norm_backward(
        first_normalized_gradient, first_centered, first_inverse_norm, first_gain
    )
    d_tokens = (dh1 + first_norm_gradient).reshape(1, tok, D)
    d_gains_part = jnp.stack([first_gain_gradient, second_gain_gradient])
    d_bias_part = dtable.reshape(H * NB)
    d_qkv_mine, d_out_mine, d_router_mine, d_gains_mine, d_bias_mine = (
        lax.psum_scatter(d_qkv_part, ("ctx", "fsdp"), scatter_dimension=0, tiled=True),
        lax.psum_scatter(d_out_part, ("ctx", "fsdp"), scatter_dimension=0, tiled=True),
        lax.psum_scatter(d_router_part, ("ctx", "fsdp"), scatter_dimension=0, tiled=True),
        lax.psum_scatter(d_gains_part, ("ctx", "fsdp"), scatter_dimension=1, tiled=True),
        lax.psum_scatter(d_bias_part, ("ctx", "fsdp"), scatter_dimension=0, tiled=True),
    )
    return (
        mixed.reshape(1, tok, D),
        d_tokens,
        d_gains_mine,
        d_bias_mine,
        d_qkv_mine,
        d_out_mine,
        d_router_mine,
        d_w_in_mine,
        d_w_out_mine,
    )


def solution(mesh):
    return jax.shard_map(
        shards,
        mesh=mesh,
        in_specs=(
            P("fsdp", "ctx", None),
            P("fsdp", "ctx", None),
            P("fsdp", "ctx", None),
            P(None, ("ctx", "fsdp")),
            P(("ctx", "fsdp")),
            P(("ctx", "fsdp"), None),
            P(("ctx", "fsdp"), None),
            P(("ctx", "fsdp"), None),
            P("ctx", None, "fsdp"),
            P("ctx", "fsdp", None),
        ),
        out_specs=(
            P("fsdp", "ctx", None),
            P("fsdp", "ctx", None),
            P(None, ("ctx", "fsdp")),
            P(("ctx", "fsdp")),
            P(("ctx", "fsdp"), None),
            P(("ctx", "fsdp"), None),
            P(("ctx", "fsdp"), None),
            P("ctx", None, "fsdp"),
            P("ctx", "fsdp", None),
        ),
        check_vma=False,
    )
```

profile of v0, /device:TPU:0, one launch (start us, length us, event | category | flops | bytes accessed | tf_op | source)
XLA Modules:
  0.0 1810.9 jit_solution(9934046982767060031)
XLA Ops:
  8.0 43.5 %all-gather = bf16[32,24,2]{1,2,0:T(2,128)(2,1)S(1)} all-gather(bf16[1,24,2]{1,2,0:T(2,128)(2,1)} %bitcast.232), channel_id=1, replica_groups=mesh['ctx'=8,'fsdp'=4] {'ctx','fsdp'}, dimensions={0}, use_global_device_ids=true | all-gather | bytes 3168 | tf_op jit(solution)/shard_map/all_gather | solution.py:82
  52.7 20.9 %all-gather.8.cloned.1.call-done = bf16[2304,768]{1,0:T(8,128)(2,1)} async-done(((bf16[72,768]{1,0:T(8,128)(2,1)}), bf16[2304,768]{1,0:T(8,128)(2,1)}) %all-gather.8.cloned.1.call-update) | async-done | bytes 3538960 | tf_op jit(solution)/shard_map/all_gather | solution.py:79
  73.5 2.4 convolution_convert_fusion.5
  76.0 2.4 convolution_convert_fusion.3
  81.0 39.1 %all-reduce = bf16[384]{0:T(512)(128)(2,1)S(1)} all-reduce(bf16[384]{0:T(512)(128)(2,1)S(1)} %dynamic-update-slice), channel_id=1, replica_groups=mesh['ctx'=8,'fsdp'=4] {'ctx','fsdp'}, use_global_device_ids=true, to_apply=%add | all-reduce | flops 384 | bytes 1536
  121.2 1.6 convolution_convert_fusion.4
  123.7 2.6 copy.116
  126.3 38.7 %all-gather.12.cloned.1.call-done = bf16[1024,768]{1,0:T(8,128)(2,1)} async-done(((bf16[128,768]{1,0:T(8,128)(2,1)}), bf16[1024,768]{1,0:T(8,128)(2,1)}) %all-gather.12.cloned.1.call-update) | async-done | bytes 1572880 | tf_op jit(solution)/shard_map/all_gather | solution.py:97
  164.9 2.7 copy.118
  168.4 13.6 while.36
  168.4 13.6 conditional.4
  169.1 3.4 fusion
  172.5 3.5 copy.108
  176.1 2.0 fusion.169
  179.5 2.5 fusion.8
  183.1 36.9 %all-gather.14.cloned.1.call-done = bf16[768,768]{1,0:T(8,128)(2,1)} async-done(((bf16[24,768]{1,0:T(8,128)(2,1)}), bf16[768,768]{1,0:T(8,128)(2,1)}) %all-gather.14.cloned.1.call-update) | async-done | bytes 1179664 | tf_op jit(solution)/shard_map/all_gather | solution.py:80
  220.0 1.8 multiply_reduce_fusion.4
  222.5 1.4 convolution_convert_fusion.1
  224.0 4.4 all-to-all-start
  229.3 53.8 %all_gather.33 = bf16[768,64]{1,0:T(8,128)(2,1)S(1)} all-gather(bf16[24,64]{1,0:T(8,128)(2,1)S(1)} %copy-done.61), channel_id=1, replica_groups=mesh['ctx'=8,'fsdp'=4] {'ctx','fsdp'}, dimensions={0}, use_global_device_ids=true | all-gather | bytes 101376 | tf_op jit(solution)/shard_map/all_gather | solution.py:81
  285.4 1.5 convolution_convert_fusion
  286.9 3.6 all-to-all-start.2
  290.5 159.0 %all-gather.16.cloned.1.call-done = bf16[8,768,3072]{2,1,0:T(8,128)(2,1)} async-done(((bf16[8,768,768]{2,1,0:T(8,128)(2,1)}), bf16[8,768,3072]{2,1,0:T(8,128)(2,1)}) %all-gather.16.cloned.1.call-update) | async-done | bytes 37748752 | tf_op jit(solution)/shard_map/all_gather | solution.py:159
  449.5 22.6 %fusion.79 = f32[8,8,8,3072]{3,2,1,0:T(8,128)} fusion(bf16[8,768,3072]{2,1,0:T(8,128)(2,1)} %all-gather.16.cloned.1.call-done, bf16[8,8,8,768]{3,2,1,0:T(8,128)(2,1)S(1)} %all-to-all-done), kind=kOutput, calls=%fused_computation.93 | convolution fusion | flops 2415919104 | bytes 44826624 | tf_op jit(solution)/shard_map/sjcd,jdf->sjcf/dot_general | solution.py:163
  473.0 203.9 %all-gather.18.cloned.1.call-done = bf16[8,3072,768]{2,1,0:T(8,128)(2,1)} async-done(((bf16[8,768,768]{2,1,0:T(8,128)(2,1)}), bf16[8,3072,768]{2,1,0:T(8,128)(2,1)}) %all-gather.18.cloned.1.call-update) | async-done | bytes 37748752 | tf_op jit(solution)/shard_map/all_gather | solution.py:160
  677.0 18.4 %fusion.91 = bf16[8,8,8,3072]{3,2,0,1:T(8,128)(2,1)S(1)} fusion(f32[8,8,8,3072]{3,2,1,0:T(8,128)} %fusion.79, bf16[8,3072,768]{2,1,0:T(8,128)(2,1)} %all-gather.18.cloned.1.call-done, bf16[8,8,8,768]{3,2,1,0:T(8,128)(2,1)} %copy-done.33), kind=kOutput, calls=%fused_computation.108 | convolution fusion | flops 2445803520 | bytes 47972352 | tf_op jit(solution)/shard_map/sjcd,jfd->sjcf/dot_general | solution.py:185
  695.3 19.1 %fusion.101 = bf16[8,8,8,768]{3,2,0,1:T(8,128)(2,1)} fusion(bf16[8,8,8,3072]{3,2,0,1:T(8,128)(2,1)S(1)} %fusion.91, bf16[8,768,3072]{2,1,0:T(8,128)(2,1)} %all-gather.16.cloned.1.call-done), kind=kOutput, calls=%fused_computation.116 | convolution fusion | flops 2416312320 | bytes 41680896 | tf_op jit(solution)/shard_map/sjcf,jdf->sjcd/dot_general | solution.py:191
  714.4 2.1 copy.130
  716.6 5.5 all-to-all-start.3
  722.1 17.2 fusion.104
  740.4 2.3 all-to-all-done.3
  742.6 4.2 all-to-all-start.1
  748.5 18.3 %all-to-all-done.1 = bf16[8,8,8,768]{3,2,1,0:T(8,128)(2,1)} async-done(((bf16[8,8,8,768]{3,2,1,0:T(8,128)(2,1)}), bf16[8,8,8,768]{3,2,1,0:T(8,128)(2,1)}, u32[]{:S(2)}, u32[]{:S(2)}) %all-to-all-start.1) | async-done | bytes 786464 | tf_op jit(solution)/shard_map/all_to_all | solution.py:169
  766.8 1.7 multiply_reduce_fusion
  768.6 2.0 multiply_reduce_fusion.2
  774.2 2.1 copy.133
  778.2 1.4 broadcast.562
  780.9 19.5 %while.37 = (s32[]{:T(128)}, f32[128,12,64]{0,2,1:T(8,128)}, bf16[1024,12,64]{0,2,1:T(8,128)(2,1)}, bf16[1024,12,64]{0,2,1:T(8,128)(2,1)}, f32[12,32]{1,0:T(8,12...) while((s32[]{:T(128)}, f32[128,12,64]{0,2,1:T(8,128)}, ...), condition=%wide.region_24.25_spmd, body=%wide.region_21.24_spmd.sunk | while | flops 871040000 | bytes 65433448 | solution.py:277
  781.4 19.1 %conditional.5 = ((f32[128,12,64]{0,2,1:T(8,128)}, bf16[1024,12,64]{0,2,1:T(8,128)(2,1)}, bf16[1024,12,64]{0,2,1:T(8,128)(2,1)}, f32[12,32]{1,0:T(8,128)S(1)})) conditional(s32[]{:T(128)} %convert_element_type.576, (f32[128,12,64]{0,2,1:T(8,128)}, bf16[1024,12,64]{0,2,1:T(8,128)(2,1)}, bf16[1024,12,64]{0,2,1:T(8,128)(2,1)}, ...), branch_computations={%region_22.22_spmd, %region_23.23_spmd} | conditional | flops 871040000 | bytes 65433128 | solution.py:269
  781.9 3.4 fusion.33
  785.4 4.0 fusion.39
  791.9 1.7 bitcast_dynamic-update-slice_fusion.1
  794.8 5.5 fusion.49
  800.5 2.8 copy.145
  803.3 1.6 copy.143
  805.0 18.1 bitcast_convert_fusion.1
  824.2 18.4 %bitcast_convert_fusion = bf16[8,3072,768]{2,1,0:T(8,128)(2,1)} fusion(bf16[8,8,8,768]{3,2,1,0:T(8,128)(2,1)S(1)} %copy-done.34, f32[8,8,8,3072]{3,2,1,0:T(8,128)} %fusion.79), kind=kOutput, calls=%fused_computation.89 | convolution fusion | flops 2448949248 | bytes 44826624 | tf_op jit(solution)/shard_map/sjcf,sjcd->jfd/dot_general | solution.py:187
  844.6 1.9 fusion.148
  847.2 38.9 %reduce-scatter.25.cloned.1.call-done = bf16[128,768]{1,0:T(8,128)(2,1)} async-done(((bf16[1024,768]{1,0:T(8,128)(2,1)}), bf16[128,768]{1,0:T(8,128)(2,1)}) %reduce-scatter.25.cloned.1.call-update) | async-done | bytes 196624
  886.1 2.9 fusion.162
  889.0 65.5 %reduce-scatter.23.cloned.1.call-done = bf16[128,768]{1,0:T(8,128)(2,1)} async-done(((bf16[1024,768]{1,0:T(8,128)(2,1)}), bf16[128,768]{1,0:T(8,128)(2,1)}) %reduce-scatter.23.cloned.1.call-update) | async-done | bytes 196624
  954.6 1.6 fusion.164
  956.3 3.2 pad_maximum_fusion
  960.3 2.0 fusion.109
  962.3 1.8 convolution_add_fusion.1
  964.2 2.3 fusion.133
  966.4 39.7 %all-reduce.4 = (f32[2,768]{1,0:T(2,128)S(1)}, f32[384]{0:T(512)S(1)}) all-reduce(f32[2,768]{1,0:T(2,128)S(1)} %pad_maximum_fusion.1, f32[384]{0:T(512)S(1)} %reshape.533), channel_id=4, replica_groups=mesh['ctx'=8,'fsdp'=4] {'ctx','fsdp'}, use_global_device_ids=true, to_apply=%region_30.31.clone | all-reduce | flops 1920 | bytes 15360
  1008.3 205.3 %reduce-scatter.19.cloned.1.call-done = bf16[8,768,768]{2,1,0:T(8,128)(2,1)} async-done(((bf16[8,768,3072]{2,1,0:T(8,128)(2,1)}), bf16[8,768,768]{2,1,0:T(8,128)(2,1)}) %reduce-scatter.19.cloned.1.call-update) | async-done | bytes 9437200 | tf_op jit(solution)/shard_map/reduce_scatter | solution.py:195
  1213.5 15.2 convert_element_type.431
  1228.7 245.0 %reduce-scatter.21.cloned.1.call-done = bf16[8,768,768]{2,1,0:T(8,128)(2,1)} async-done(((bf16[8,3072,768]{2,1,0:T(8,128)(2,1)}), bf16[8,768,768]{2,1,0:T(8,128)(2,1)}) %reduce-scatter.21.cloned.1.call-update) | async-done | bytes 9437200 | tf_op jit(solution)/shard_map/reduce_scatter | solution.py:198
  1473.7 12.2 convert_element_type.433
  1485.9 88.9 %reduce-scatter.27.cloned.1.call-done = f32[24,64]{1,0:T(8,128)} async-done(((f32[768,64]{1,0:T(8,128)}), f32[24,64]{1,0:T(8,128)}) %reduce-scatter.27.cloned.1.call-update) | async-done | bytes 6160
  1574.8 104.4 %reduce-scatter.17.cloned.1.call-done = f32[24,768]{1,0:T(8,128)} async-done(((f32[768,768]{1,0:T(8,128)}), f32[24,768]{1,0:T(8,128)}) %reduce-scatter.17.cloned.1.call-update) | async-done | bytes 73744 | tf_op jit(solution)/shard_map/reduce_scatter | solution.py:315
  1679.3 124.9 %reduce-scatter.15.cloned.1.call-done = f32[72,768]{1,0:T(8,128)} async-done(((f32[2304,768]{1,0:T(8,128)}), f32[72,768]{1,0:T(8,128)}) %reduce-scatter.15.cloned.1.call-update) | async-done | bytes 221200 | tf_op jit(solution)/shard_map/reduce_scatter | solution.py:314
  (250 shorter events, 35.7 us)
Async XLA Ops:
  7.2 66.4 %all-gather.8.cloned.1.call-start = ((), (), s32[]{:S(2)}) async-start(), calls=%async_computation.11 | async-start | bytes 3649536 | tf_op jit(solution)/shard_map/all_gather | solution.py:79
  7.9 115.8 %all-gather.10.cloned.1.call-start = ((), (), s32[]{:S(2)}) async-start(), calls=%async_computation.12 | async-start | bytes 1769472 | tf_op jit(solution)/shard_map/all_gather | solution.py:96
  51.6 69.6 %copy-start.44 = (f32[768]{0:T(1024)}, f32[768]{0:T(1024)S(1)}, u32[]{:S(2)}) copy-start(f32[768]{0:T(1024)S(1)} %get-tuple-element.551) | copy-start | bytes 9220
  51.6 170.2 %copy-start.46 = (f32[768]{0:T(1024)}, f32[768]{0:T(1024)S(1)}, u32[]{:S(2)}) copy-start(f32[768]{0:T(1024)S(1)} %get-tuple-element.550) | copy-start | bytes 9220
  52.6 68.6 %copy-start.57 = (f32[128]{0:T(128)}, f32[128]{0:T(128)S(1)}, u32[]{:S(2)}) copy-start(f32[128]{0:T(128)S(1)} %add_rsqrt_fusion.1) | copy-start | bytes 1540
  76.0 89.0 %all-gather.12.cloned.1.call-start = ((), (), s32[]{:S(2)}) async-start(), calls=%async_computation.13 | async-start | bytes 1769472 | tf_op jit(solution)/shard_map/all_gather | solution.py:97
  78.5 141.5 %all-gather.14.cloned.1.call-start = ((), (), s32[]{:S(2)}) async-start(), calls=%async_computation.14 | async-start | bytes 1216512 | tf_op jit(solution)/shard_map/all_gather | solution.py:80
  79.1 370.5 %all-gather.16.cloned.1.call-start = ((), (), s32[]{:S(2)}) async-start(), calls=%async_computation.15 | async-start | bytes 47185920 | tf_op jit(solution)/shard_map/all_gather | solution.py:159
  79.7 41.6 %copy-start.8 = (bf16[1,128,768]{2,1,0:T(8,128)(2,1)S(1)}, bf16[1,128,768]{2,1,0:T(8,128)(2,1)}, u32[]{:S(2)}) copy-start(bf16[1,128,768]{2,1,0:T(8,128)(2,1)} %param.18) | copy-start | bytes 589828
  79.7 597.3 %all-gather.18.cloned.1.call-start = ((), (), s32[]{:S(2)}) async-start(), calls=%async_computation.16 | async-start | bytes 47185920 | tf_op jit(solution)/shard_map/all_gather | solution.py:160
  80.4 148.8 %copy-start.28 = (s32[1,128,2]{2,1,0:T(8,128)}, s32[1,128,2]{2,1,0:T(8,128)S(1)}, u32[]{:S(2)}) copy-start(s32[1,128,2]{2,1,0:T(8,128)S(1)} %copy.119) | copy-start | bytes 3076
  121.2 46.4 %copy-start.53 = (s32[256]{0:T(256)}, s32[256]{0:T(256)S(1)}, u32[]{:S(2)}) copy-start(s32[256]{0:T(256)S(1)} %fusion.153) | copy-start | bytes 3076
  182.1 41.9 %copy-start.37 = (bf16[12,32]{1,0:T(8,128)(2,1)}, bf16[12,32]{1,0:T(8,128)(2,1)S(1)}, u32[]{:S(2)}) copy-start(bf16[12,32]{1,0:T(8,128)(2,1)S(1)} %get-tuple-element.926) | copy-start | bytes 2308
  183.1 40.9 %copy-start.19 = (bf16[12,128,64]{1,2,0:T(8,128)(2,1)}, bf16[12,128,64]{1,2,0:T(8,128)(2,1)S(1)}, u32[]{:S(2)}) copy-start(bf16[12,128,64]{1,2,0:T(8,128)(2,1)S(1)} %divide_convert_fusion) | copy-start | bytes 589828
  220.0 8.4 copy-start.35
  221.9 61.2 %copy-start.22 = (bf16[128,768]{1,0:T(8,128)(2,1)}, bf16[128,768]{1,0:T(8,128)(2,1)S(1)}, u32[]{:S(2)}) copy-start(bf16[128,768]{1,0:T(8,128)(2,1)S(1)} %multiply_convert_fusion.3) | copy-start | bytes 589828
  222.5 6.8 copy-start.61
  224.0 62.9 %all-to-all-start = ((bf16[8,8,8,768]{3,2,1,0:T(8,128)(2,1)}), bf16[8,8,8,768]{3,2,1,0:T(8,128)(2,1)S(1)}, u32[]{:S(2)}, u32[]{:S(2)}) async-start(bf16[8,8,8,768]{3,2,1,0:T(8,128)(2,1)} %bitcast.23), calls=%async_computation | async-start | bytes 1572864 | tf_op jit(solution)/shard_map/all_to_all | solution.py:157
  228.4 58.5 %copy-start.30 = (f32[128,768]{1,0:T(8,128)}, f32[128,768]{1,0:T(8,128)S(1)}, u32[]{:S(2)}) copy-start(f32[128,768]{1,0:T(8,128)S(1)} %bitcast_convert_fusion.2) | copy-start | bytes 1179652
  229.3 54.1 %copy-start.55 = (s32[128,2]{0,1:T(2,128)}, s32[128,2]{0,1:T(2,128)S(1)}, u32[]{:S(2)}) copy-start(s32[128,2]{0,1:T(2,128)S(1)} %copy.120) | copy-start | bytes 3076
  283.1 189.0 %copy-start.26 = (bf16[768,64]{1,0:T(8,128)(2,1)}, bf16[768,64]{1,0:T(8,128)(2,1)S(1)}, u32[]{:S(2)}) copy-start(bf16[768,64]{1,0:T(8,128)(2,1)S(1)} %all_gather.33) | copy-start | bytes 294916
  286.9 185.2 %copy-start.24 = (bf16[8,8,8,768]{3,2,1,0:T(8,128)(2,1)}, bf16[8,8,8,768]{3,2,1,0:T(8,128)(2,1)S(1)}, u32[]{:S(2)}) copy-start(bf16[8,8,8,768]{3,2,1,0:T(8,128)(2,1)S(1)} %all-to-all-done) | copy-start | bytes 2359300
  286.9 185.2 %all-to-all-start.2 = ((bf16[8,8,8,768]{3,2,1,0:T(8,128)(2,1)}), bf16[8,8,8,768]{3,2,1,0:T(8,128)(2,1)S(1)}, u32[]{:S(2)}, u32[]{:S(2)}) async-start(bf16[8,8,8,768]{3,2,1,0:T(8,128)(2,1)} %bitcast.35), calls=%async_computation.2 | async-start | bytes 1572864 | tf_op jit(solution)/shard_map/all_to_all | solution.py:184
  695.3 19.1 %copy-start.18 = (bf16[8,8,8,3072]{3,2,0,1:T(8,128)(2,1)}, bf16[8,8,8,3072]{3,2,0,1:T(8,128)(2,1)S(1)}, u32[]{:S(2)}) copy-start(bf16[8,8,8,3072]{3,2,0,1:T(8,128)(2,1)S(1)} %fusion.91) | copy-start | bytes 9437188
  716.6 26.1 %all-to-all-start.3 = ((bf16[8,8,8,768]{3,2,1,0:T(8,128)(2,1)}), bf16[8,8,8,768]{3,2,1,0:T(8,128)(2,1)S(1)}, u32[]{:S(2)}, u32[]{:S(2)}) async-start(bf16[8,8,8,768]{3,2,1,0:T(8,128)(2,1)} %copy.130), calls=%async_computation.3 | async-start | bytes 1572864 | tf_op jit(solution)/shard_map/all_to_all | solution.py:202
  739.3 7.6 copy-start.54
  739.3 7.8 copy-start.29
  739.3 7.9 copy-start.20
  739.3 27.5 %copy-start.31 = (f32[128,768]{1,0:T(8,128)S(1)}, f32[128,768]{1,0:T(8,128)}, u32[]{:S(2)}) copy-start(f32[128,768]{1,0:T(8,128)} %copy-done.30) | copy-start | bytes 1179652
  739.3 27.5 %copy-start.65 = (f32[128,2]{0,1:T(2,128)S(1)}, f32[128,2]{0,1:T(2,128)}, u32[]{:S(2)}) copy-start(f32[128,2]{0,1:T(2,128)} %copy-done.64) | copy-start | bytes 3076
  739.3 29.2 %copy-start.49 = (f32[128,2]{0,1:T(2,128)S(1)}, f32[128,2]{0,1:T(2,128)}, u32[]{:S(2)}) copy-start(f32[128,2]{0,1:T(2,128)} %copy-done.48) | copy-start | bytes 3076
  739.3 29.2 %copy-start.52 = (f32[128]{0:T(128)S(1)}, f32[128]{0:T(128)}, u32[]{:S(2)}) copy-start(f32[128]{0:T(128)} %copy-done.51) | copy-start | bytes 1540
  739.3 29.2 %copy-start.60 = (f32[128]{0:T(128)S(1)}, f32[128]{0:T(128)}, u32[]{:S(2)}) copy-start(f32[128]{0:T(128)} %copy-done.59) | copy-start | bytes 1540
  739.3 29.2 %copy-start.56 = (s32[128,2]{0,1:T(2,128)S(1)}, s32[128,2]{0,1:T(2,128)}, u32[]{:S(2)}) copy-start(s32[128,2]{0,1:T(2,128)} %copy-done.55) | copy-start | bytes 3076
  739.4 29.2 %copy-start.27 = (bf16[768,64]{1,0:T(8,128)(2,1)S(1)}, bf16[768,64]{1,0:T(8,128)(2,1)}, u32[]{:S(2)}) copy-start(bf16[768,64]{1,0:T(8,128)(2,1)} %copy-done.26) | copy-start | bytes 294916
  739.4 29.2 %copy-start.47 = (f32[768]{0:T(1024)S(1)}, f32[768]{0:T(1024)}, u32[]{:S(2)}) copy-start(f32[768]{0:T(1024)} %copy-done.46) | copy-start | bytes 9220
  739.4 29.2 %copy-start.63 = (f32[128]{0:T(128)S(1)}, f32[128]{0:T(128)}, u32[]{:S(2)}) copy-start(f32[128]{0:T(128)} %copy-done.62) | copy-start | bytes 1540
  740.4 30.2 %copy-start.36 = (bf16[1,128,768]{2,1,0:T(8,128)(2,1)S(1)}, bf16[1,128,768]{2,1,0:T(8,128)(2,1)}, u32[]{:S(2)}) copy-start(bf16[1,128,768]{2,1,0:T(8,128)(2,1)} %param.20) | copy-start | bytes 589828
  742.6 24.2 %all-to-all-start.1 = ((bf16[8,8,8,768]{3,2,1,0:T(8,128)(2,1)}), bf16[8,8,8,768]{3,2,1,0:T(8,128)(2,1)}, u32[]{:S(2)}, u32[]{:S(2)}) async-start(bf16[8,8,8,768]{3,2,1,0:T(8,128)(2,1)} %copy.126), calls=%async_computation.1 | async-start | bytes 1572864 | tf_op jit(solution)/shard_map/all_to_all | solution.py:169
  746.9 139.3 %reduce-scatter.25.cloned.1.call-start = ((), (), s32[]{:S(2)}) async-start(), calls=%async_computation.22 | async-start | bytes 1769472
  747.3 24.8 %copy-start.17 = (bf16[768,768]{1,0:T(8,128)(2,1)S(1)}, bf16[768,768]{1,0:T(8,128)(2,1)}, u32[]{:S(2)}) copy-start(bf16[768,768]{1,0:T(8,128)(2,1)} %all-gather.14.cloned.1.call-done) | copy-start | bytes 3538948
  768.6 2.7 copy-start.42
  773.4 7.5 copy-start
  773.4 7.5 copy-start.2
  773.4 7.5 copy-start.38
  785.4 4.1 copy-start.3
  791.7 1.9 copy-start.13
  794.8 5.6 copy-start.14
  800.5 4.4 copy-start.39
  800.5 2.8 copy-start.12
  803.3 151.3 %reduce-scatter.23.cloned.1.call-start = ((), (), s32[]{:S(2)}) async-start(), calls=%async_computation.21 | async-start | bytes 1769472
  804.9 408.6 %reduce-scatter.19.cloned.1.call-start = ((), (), s32[]{:S(2)}) async-start(), calls=%async_computation.19 | async-start | bytes 47185920 | tf_op jit(solution)/shard_map/reduce_scatter | solution.py:195
  823.1 650.6 %reduce-scatter.21.cloned.1.call-start = ((), (), s32[]{:S(2)}) async-start(), calls=%async_computation.20 | async-start | bytes 47185920 | tf_op jit(solution)/shard_map/reduce_scatter | solution.py:198
  842.6 2.0 copy-start.16
  842.6 2.0 copy-start.21
  842.7 3.9 copy-start.6
  842.7 732.2 %reduce-scatter.27.cloned.1.call-start = ((), (), s32[]{:S(2)}) async-start(), calls=%async_computation.23 | async-start | bytes 405504
  844.5 2.1 copy-start.9
  844.5 2.1 copy-start.45
  844.6 2.1 copy-start.58
  844.6 834.7 %reduce-scatter.17.cloned.1.call-start = ((), (), s32[]{:S(2)}) async-start(), calls=%async_computation.18 | async-start | bytes 2433024 | tf_op jit(solution)/shard_map/reduce_scatter | solution.py:315
  846.5 957.6 %reduce-scatter.15.cloned.1.call-start = ((), (), s32[]{:S(2)}) async-start(), calls=%async_computation.17 | async-start | bytes 7299072 | tf_op jit(solution)/shard_map/reduce_scatter | solution.py:314
  959.5 2.8 copy-start.32
  959.5 4.6 copy-start.41
  (21 other events, 19.9 us)
Sparse Core Ops, SparseCore 0:
  10.9 62.5 all-gather.7
  76.3 43.2 all-gather.9
  122.4 42.5 all-gather.11
  167.7 52.2 all-gather.13
  221.4 228.0 all-gather.15
  450.9 225.9 all-gather.17
  803.4 82.7 reduce-scatter.24
  890.1 64.4 reduce-scatter.22
  957.2 256.3 reduce-scatter.18
  1216.0 257.6 reduce-scatter.20
  1479.2 95.5 reduce-scatter.26
  1580.6 98.6 reduce-scatter.16
  1685.5 118.5 reduce-scatter.14
where the time goes:
time: 1820 us; the launch traced here: 1810 us
  waiting for transfers between devices  1360 us (75%)
  blocking collectives  176 us (10%)
  matrix products  170 us (9%)
  other arithmetic  38.3 us (2%)
  local copies, waits for them, and re-layouts  37.6 us (2%)
  starting transfers between devices  18.2 us (1%)
    reduce_scatter x1, waiting for transfers between devices, shards(): lax.psum_scatter(d_w_out_whole.astype(jnp.bfloat16), 'fsdp', scatter_dime...  245 us
    reduce_scatter x1, waiting for transfers between devices, shards(): lax.psum_scatter(d_w_in_whole.astype(jnp.bfloat16), 'fsdp', scatter_dimen...  205 us
    all_gather x1, waiting for transfers between devices, shards(): lax.all_gather(w_out, 'fsdp', axis=1, tiled=True)  204 us
    unnamed x16, waiting for transfers between devices  196 us
    all_gather x1, waiting for transfers between devices, shards(): lax.all_gather(w_in, 'fsdp', axis=2, tiled=True)  159 us
    reduce_scatter x1, waiting for transfers between devices, shards(): lax.psum_scatter(d_qkv_part, ('ctx', 'fsdp'), scatter_dimension=0, tiled=...  125 us
    reduce_scatter x1, waiting for transfers between devices, shards(): lax.psum_scatter(d_out_part, ('ctx', 'fsdp'), scatter_dimension=0, tiled=...  104 us
    unnamed x2, blocking collectives  78.8 us
  transfers between devices with their start and end apart: 17, of which 14 were waited for; matrix products, arithmetic and copies ran while one was open for 9% of the time, Pallas kernels for 0%

commit v1 on v0

--- a/solution.py
+++ b/solution.py
@@ -75,13 +75,33 @@
     per_dev = w_in.shape[0]
     scale = 1.0 / math.sqrt(DH)
     kblk = math.gcd(seq_len, 512)
-    qkv_full, out_full, router_full, gains_full, bias_full = (
-        lax.all_gather(attn_qkv, ("ctx", "fsdp"), axis=0, tiled=True),
-        lax.all_gather(attn_out, ("ctx", "fsdp"), axis=0, tiled=True),
-        lax.all_gather(router, ("ctx", "fsdp"), axis=0, tiled=True),
-        lax.all_gather(gains, ("ctx", "fsdp"), axis=1, tiled=True),
-        lax.all_gather(rel_bias, ("ctx", "fsdp"), axis=0, tiled=True),
-    )
+    axes = ("ctx", "fsdp")
+    n_fsdp = lax.axis_size("fsdp")
+    n_dev = n_ctx * n_fsdp
+    qkv_rows, out_rows = attn_qkv.shape[0], attn_out.shape[0]
+    tail_sizes = (router.size, gains.size, rel_bias.size)
+    tail_used = sum(tail_sizes)
+    tail_rows = -(-tail_used // D)
+    head_rows = qkv_rows + out_rows
+    pack_rows = -(-(head_rows + tail_rows) // 8) * 8
+    tail = jnp.concatenate([router.reshape(-1), gains.reshape(-1), rel_bias.reshape(-1)])
+    tail = jnp.pad(tail, (0, (pack_rows - head_rows) * D - tail_used))
+    weights_pack = jnp.concatenate(
+        [attn_qkv, attn_out, tail.reshape(pack_rows - head_rows, D)], axis=0
+    )
+    weights_all = lax.all_gather(weights_pack, axes, axis=0, tiled=False)
+    qkv_full = weights_all[:, :qkv_rows].reshape(n_dev * qkv_rows, D)
+    out_full = weights_all[:, qkv_rows:head_rows].reshape(n_dev * out_rows, D)
+    tails = weights_all[:, head_rows:].reshape(n_dev, -1)
+    cut_one = tail_sizes[0] + tail_sizes[1]
+    router_full = tails[:, : tail_sizes[0]].reshape(D, E)
+    gains_full = (
+        tails[:, tail_sizes[0] : cut_one]
+        .reshape(n_dev, 2, gains.shape[1])
+        .transpose(1, 0, 2)
+        .reshape(2, D)
+    )
+    bias_full = tails[:, cut_one:tail_used].reshape(H * NB)
     w_qkv = qkv_full.reshape(3, D, D)
     bias_table = bias_full.reshape(H, NB)
     first_gain = gains_full[0].astype(single_float)
@@ -92,10 +112,8 @@
     q = jnp.dot(first_normalized, w_qkv[0], preferred_element_type=single_float).astype(bfloat_half)
     k = jnp.dot(first_normalized, w_qkv[1], preferred_element_type=single_float).astype(bfloat_half)
     v = jnp.dot(first_normalized, w_qkv[2], preferred_element_type=single_float).astype(bfloat_half)
-    keys_all, values_all = (
-        lax.all_gather(k, "ctx", axis=0, tiled=True),
-        lax.all_gather(v, "ctx", axis=0, tiled=True),
-    )
+    keys_values = lax.all_gather(jnp.concatenate([k, v], axis=1), "ctx", axis=0, tiled=True)
+    keys_all, values_all = keys_values[:, :D], keys_values[:, D:]
     qheads = q.reshape(tok, H, DH)
     kheads = keys_all.reshape(seq_len, H, DH)
     vheads = values_all.reshape(seq_len, H, DH)
@@ -148,66 +166,52 @@
     table_disp = (target[:, None] == jnp.arange(E * CAP, dtype=jnp.int32)[None, :]).astype(
         bfloat_half
     )
+    dy = cotangent.reshape(tok, D).astype(single_float)
     doubled = jnp.repeat(second_normalized, 2, axis=0)
+    dpicked = (gate[:, :, None] * dy[:, None, :]).astype(bfloat_half).reshape(2 * tok, D)
     packed = (
-        jnp.einsum("ac,ad->cd", table_disp, doubled, preferred_element_type=single_float)
+        jnp.einsum(
+            "ac,ad->cd",
+            table_disp,
+            jnp.concatenate([doubled, dpicked], axis=1),
+            preferred_element_type=single_float,
+        )
         .astype(bfloat_half)
-        .reshape(n_ctx, per_dev, CAP, D)
+        .reshape(n_ctx, per_dev, CAP, 2 * D)
     )
     received = lax.all_to_all(packed, "ctx", split_axis=0, concat_axis=0, tiled=True)
-    w_in_full, w_out_full = (
-        lax.all_gather(w_in, "fsdp", axis=2, tiled=True),
-        lax.all_gather(w_out, "fsdp", axis=1, tiled=True),
-    )
+    rows_one = n_ctx * CAP
+    received = received.transpose(1, 0, 2, 3).reshape(per_dev, rows_one, 2 * D)
+    received_all = lax.all_gather(received, "fsdp", axis=0, tiled=False)
+    received_all = received_all.transpose(1, 0, 2, 3).reshape(per_dev, n_fsdp * rows_one, 2 * D)
+    buf, dbuf = received_all[:, :, :D], received_all[:, :, D:]
     hid, slope = gelu_parts(
-        jnp.einsum("sjcd,jdf->sjcf", received, w_in_full, preferred_element_type=single_float)
+        jnp.einsum("jcd,jdf->jcf", buf, w_in, preferred_element_type=single_float)
     )
     hid_bf = hid.astype(bfloat_half)
-    expert_out = jnp.einsum(
-        "sjcf,jfd->sjcd", hid_bf, w_out_full, preferred_element_type=single_float
-    ).astype(bfloat_half)
-    returned = lax.all_to_all(expert_out, "ctx", split_axis=0, concat_axis=0, tiled=True)
-    picked = jnp.einsum(
-        "ac,cd->ad", table_disp, returned.reshape(E * CAP, D), preferred_element_type=single_float
-    ).reshape(tok, 2, D)
+    dhid = jnp.einsum("jcd,jfd->jcf", dbuf, w_out, preferred_element_type=single_float)
+    dpre = (dhid * slope).astype(bfloat_half)
+    expert_part = jnp.einsum("jcf,jfd->jcd", hid_bf, w_out, preferred_element_type=single_float)
+    dreturn_part = jnp.einsum("jcf,jdf->jcd", dpre, w_in, preferred_element_type=single_float)
+    part = jnp.concatenate(
+        [expert_part.astype(bfloat_half), dreturn_part.astype(bfloat_half)], axis=-1
+    )
+    part = part.reshape(per_dev, n_fsdp, rows_one, 2 * D).transpose(1, 0, 2, 3)
+    part = part.reshape(n_fsdp * per_dev * rows_one, 2 * D)
+    summed = lax.psum_scatter(part, "fsdp", scatter_dimension=0, tiled=True)
+    d_w_out_mine = jnp.einsum("jcf,jcd->jfd", hid_bf, dbuf, preferred_element_type=single_float)
+    d_w_in_mine = jnp.einsum("jcd,jcf->jdf", buf, dpre, preferred_element_type=single_float)
+    summed = summed.reshape(per_dev, n_ctx, CAP, 2 * D).transpose(1, 0, 2, 3)
+    returned = lax.all_to_all(summed, "ctx", split_axis=0, concat_axis=0, tiled=True)
+    both = jnp.einsum(
+        "ac,cd->ad", table_disp, returned.reshape(E * CAP, 2 * D), preferred_element_type=single_float
+    ).reshape(tok, 2, 2 * D)
+    picked = both[:, :, :D]
     mixed = (first_hidden + jnp.sum(gate[:, :, None] * picked, axis=1)).astype(bfloat_half)
-    dy = cotangent.reshape(tok, D).astype(single_float)
     dgate = jnp.sum(dy[:, None, :] * picked, axis=-1)
     dchosen = gate * (dgate - jnp.sum(gate * dgate, axis=-1, keepdims=True))
     dlogits = jnp.sum(chosen_mask * dchosen[:, :, None], axis=1).astype(bfloat_half)
-    dpicked = (gate[:, :, None] * dy[:, None, :]).astype(bfloat_half).reshape(2 * tok, D)
-    dpacked = (
-        jnp.einsum("ac,ad->cd", table_disp, dpicked, preferred_element_type=single_float)
-        .astype(bfloat_half)
-        .reshape(n_ctx, per_dev, CAP, D)
-    )
-    dreceived = lax.all_to_all(dpacked, "ctx", split_axis=0, concat_axis=0, tiled=True)
-    dhid = jnp.einsum("sjcd,jfd->sjcf", dreceived, w_out_full, preferred_element_type=single_float)
-    dpre = (dhid * slope).astype(bfloat_half)
-    d_w_out_whole = jnp.einsum(
-        "sjcf,sjcd->jfd", hid_bf, dreceived, preferred_element_type=single_float
-    )
-    d_w_in_whole = jnp.einsum("sjcd,sjcf->jdf", received, dpre, preferred_element_type=single_float)
-    dreturn = jnp.einsum(
-        "sjcf,jdf->sjcd", dpre, w_in_full, preferred_element_type=single_float
-    ).astype(bfloat_half)
-    d_w_in_mine, d_w_out_mine = (
-        lax.psum_scatter(
-            d_w_in_whole.astype(jnp.bfloat16), "fsdp", scatter_dimension=2, tiled=True
-        ).astype(jnp.float32),
-        lax.psum_scatter(
-            d_w_out_whole.astype(jnp.bfloat16), "fsdp", scatter_dimension=1, tiled=True
-        ).astype(jnp.float32),
-    )
-    dback = lax.all_to_all(dreturn, "ctx", split_axis=0, concat_axis=0, tiled=True).reshape(
-        E * CAP, D
-    )
-    second_normalized_gradient = jnp.sum(
-        jnp.einsum("ac,cd->ad", table_disp, dback, preferred_element_type=single_float).reshape(
-            tok, 2, D
-        ),
-        axis=1,
-    )
+    second_normalized_gradient = jnp.sum(both[:, :, D:], axis=1)
     second_normalized_gradient = second_normalized_gradient + jnp.einsum(
         "te,de->td", dlogits, router_full, preferred_element_type=single_float
     )
@@ -275,19 +279,15 @@
         jnp.zeros((H, NB), single_float),
     )
     dq, dk_all, dv_all, dtable = lax.fori_loop(0, seq_len // kblk, backward_step, init_back)
-    dk_mine, dv_mine = (
-        lax.psum_scatter(
-            dk_all.reshape(seq_len, D).astype(jnp.bfloat16), "ctx", scatter_dimension=0, tiled=True
-        ).astype(jnp.float32),
-        lax.psum_scatter(
-            dv_all.reshape(seq_len, D).astype(jnp.bfloat16), "ctx", scatter_dimension=0, tiled=True
-        ).astype(jnp.float32),
-    )
-    grads_in = (
-        dq.reshape(tok, D).astype(bfloat_half),
-        dk_mine.astype(bfloat_half),
-        dv_mine.astype(bfloat_half),
-    )
+    dkv = jnp.concatenate(
+        [
+            dk_all.reshape(seq_len, D).astype(bfloat_half),
+            dv_all.reshape(seq_len, D).astype(bfloat_half),
+        ],
+        axis=1,
+    )
+    dkv_mine = lax.psum_scatter(dkv, "ctx", scatter_dimension=0, tiled=True)
+    grads_in = (dq.reshape(tok, D).astype(bfloat_half), dkv_mine[:, :D], dkv_mine[:, D:])
     d_qkv_part = jnp.concatenate(
         [
             jnp.einsum("td,te->de", first_normalized, part, preferred_element_type=single_float)
@@ -309,14 +309,31 @@
     )
     d_tokens = (dh1 + first_norm_gradient).reshape(1, tok, D)
     d_gains_part = jnp.stack([first_gain_gradient, second_gain_gradient])
-    d_bias_part = dtable.reshape(H * NB)
-    d_qkv_mine, d_out_mine, d_router_mine, d_gains_mine, d_bias_mine = (
-        lax.psum_scatter(d_qkv_part, ("ctx", "fsdp"), scatter_dimension=0, tiled=True),
-        lax.psum_scatter(d_out_part, ("ctx", "fsdp"), scatter_dimension=0, tiled=True),
-        lax.psum_scatter(d_router_part, ("ctx", "fsdp"), scatter_dimension=0, tiled=True),
-        lax.psum_scatter(d_gains_part, ("ctx", "fsdp"), scatter_dimension=1, tiled=True),
-        lax.psum_scatter(d_bias_part, ("ctx", "fsdp"), scatter_dimension=0, tiled=True),
-    )
+    d_tail = jnp.concatenate(
+        [
+            d_router_part.reshape(n_dev, tail_sizes[0]),
+            d_gains_part.reshape(2, n_dev, gains.shape[1])
+            .transpose(1, 0, 2)
+            .reshape(n_dev, tail_sizes[1]),
+            dtable.reshape(n_dev, tail_sizes[2]),
+        ],
+        axis=1,
+    )
+    d_tail = jnp.pad(d_tail, ((0, 0), (0, (pack_rows - head_rows) * D - tail_used)))
+    d_pack = jnp.concatenate(
+        [
+            d_qkv_part.reshape(n_dev, qkv_rows, D),
+            d_out_part.reshape(n_dev, out_rows, D),
+            d_tail.reshape(n_dev, pack_rows - head_rows, D),
+        ],
+        axis=1,
+    )
+    d_mine = lax.psum_scatter(d_pack, axes, scatter_dimension=0, tiled=False)
+    d_qkv_mine, d_out_mine = d_mine[:qkv_rows], d_mine[qkv_rows:head_rows]
+    tail_mine = d_mine[head_rows:].reshape(-1)
+    d_router_mine = tail_mine[: tail_sizes[0]].reshape(router.shape)
+    d_gains_mine = tail_mine[tail_sizes[0] : cut_one].reshape(gains.shape)
+    d_bias_mine = tail_mine[cut_one:tail_used]
     return (
         mixed.reshape(1, tok, D),
         d_tokens,

time: 1820 us -> 746 us (0.41)
  waiting for transfers between devices: 1360 us -> 414 us
  blocking collectives: 176 us -> 54.7 us
  matrix products: 170 us -> 112 us
  local copies, waits for them, and re-layouts: 37.6 us -> 90.4 us
    reduce_scatter x4 -> x2, waiting for transfers between devices: 680 us -> 171 us  [the longest x1 112 us: shards(): d_mine = lax.psum_scatter(d_pack, axes, scatter_dimension=0, tiled=False)]
    all_gather x6 -> x3, waiting for transfers between devices: 459 us -> 132 us  [the longest x1 66.2 us: shards(): weights_all = lax.all_gather(weights_pack, axes, axis=0, tiled=False)]
    unnamed x16 -> x7, waiting for transfers between devices: 196 us -> 77.3 us
    all_gather x2 -> x0, blocking collectives: 97.2 us -> none  [the longest x1 53.8 us: shards(): lax.all_gather(router, ('ctx', 'fsdp'), axis=0, tiled=True)]
    unnamed x2 -> x0, blocking collectives: 78.8 us -> none
    all_to_all x0 -> x1, blocking collectives: none -> 54.7 us  [shards(): lax.all_to_all(packed, 'ctx', split_axis=0, concat_axis=0, tiled=True)]
    dot_general x10 -> x8, matrix products: 120 us -> 66.6 us  [the longest x1 13.5 us: shards(): jnp.einsum('jcf,jcd->jfd', hid_bf, dbuf, preferred_element_type=single_fl...]
    convert_element_type x2, other arithmetic: 27.4 us -> 0.71 us  [the longest x1 0.6 us: shards(): second_gain = gains_full[1].astype(single_float)]
  transfers between devices with their start and end apart: 17 -> 7, of which waited for: 14 -> 7; matrix products, arithmetic and copies ran while one was open for 9% -> 11% of each run, Pallas kernels for 0% -> 0%
where the time goes in v1:
time: 746 us; the launch traced here: 735 us
  waiting for transfers between devices  414 us (55%)
  matrix products  112 us (15%)
  local copies, waits for them, and re-layouts  90.4 us (12%)
  blocking collectives  54.7 us (7%)
  other arithmetic  42.4 us (6%)
  between operations  15.2 us (2%)
    reduce_scatter x1, waiting for transfers between devices, shards(): d_mine = lax.psum_scatter(d_pack, axes, scatter_dimension=0, tiled=False)  112 us
    unnamed x7, waiting for transfers between devices  77.3 us
    all_gather x1, waiting for transfers between devices, shards(): weights_all = lax.all_gather(weights_pack, axes, axis=0, tiled=False)  66.2 us
    reduce_scatter x1, waiting for transfers between devices, shards(): summed = lax.psum_scatter(part, 'fsdp', scatter_dimension=0, tiled=True)  59 us
    all_to_all x1, blocking collectives, shards(): lax.all_to_all(packed, 'ctx', split_axis=0, concat_axis=0, tiled=True)  54.7 us
    all_gather x1, waiting for transfers between devices, shards(): received_all = lax.all_gather(received, 'fsdp', axis=0, tiled=False)  45.2 us
    all_to_all x1, waiting for transfers between devices, shards(): lax.all_to_all(summed, 'ctx', split_axis=0, concat_axis=0, tiled=True)  34.6 us
    all_gather x1, waiting for transfers between devices, shards(): lax.all_gather(jnp.concatenate([k, v], axis=1), 'ctx', axis=0, tiled=True)  20.2 us
  transfers between devices with their start and end apart: 7, of which 7 were waited for; matrix products, arithmetic and copies ran while one was open for 11% of the time, Pallas kernels for 0%

profile of v1, /device:TPU:0, one launch (start us, length us, event | category | flops | bytes accessed | tf_op | source)
XLA Modules:
  0.0 735.0 jit_solution(9482197660551063213)
XLA Ops:
  9.5 1.6 pad_maximum_fusion.5
  12.8 66.2 %all-gather.9.cloned.1.call-done = bf16[3328,768]{1,0:T(8,128)(2,1)} async-done(((bf16[104,768]{1,0:T(8,128)(2,1)}), bf16[3328,768]{1,0:T(8,128)(2,1)}) %all-gather.9.cloned.1.call-update) | async-done | bytes 5111824 | tf_op jit(solution)/shard_map/all_gather | solution.py:92
  79.0 1.8 slice.128
  80.8 2.2 slice.131
  83.0 2.7 copy.161
  94.1 1.5 eq.105
  95.7 1.5 eq.109
  100.0 2.0 reduce-window.6
  102.0 1.6 slice_reduce_fusion.1
  109.0 2.6 mul.308
  115.5 1.8 slice.140
  117.3 2.4 slice.138
  122.4 1.8 copy.133
  126.3 1.7 reshape.626
  128.0 2.0 convolution_convert_fusion.4
  131.1 20.2 %all-gather.5.cloned.1.call-done = bf16[1024,1536]{1,0:T(8,128)(2,1)} async-done(((bf16[128,1536]{1,0:T(8,128)(2,1)}), bf16[1024,1536]{1,0:T(8,128)(2,1)}) %all-gather.5.cloned.1.call-update) | async-done | bytes 3145744 | tf_op jit(solution)/shard_map/all_gather | solution.py:115
  151.3 2.1 fusion.149
  153.4 1.7 copy.129
  155.1 1.6 copy.126
  157.5 14.9 %while.36 = (s32[]{:T(128)}, f32[12,128]{1,0:T(8,128)S(1)}, f32[12,128]{1,0:T(8,128)S(1)}, f32[12,128,64]{1,2,0:T(8,128)}, s32[]{:T(128)}, /*index=5*/s32[]{:T(1...) while((s32[]{:T(128)}, f32[12,128]{1,0:T(8,128)S(1)}, ...), condition=%wide.region_6.7_spmd, body=%wide.region_1.6_spmd.sunk | while | flops 263786112 | bytes 32158300 | solution.py:151
  157.5 14.9 %conditional.4 = ((f32[12,128]{1,0:T(8,128)S(1)}, f32[12,128]{1,0:T(8,128)S(1)}, f32[12,128,64]{1,2,0:T(8,128)})) conditional(s32[]{:T(128)} %convert_element_type.573, (f32[12,128]{1,0:T(8,128)S(1)}, f32[12,128]{1,0:T(8,128)S(1)}, f32[12,128,64]{1,2,0:T(8,128)}) %tuple.87, (s32[]{:T(128)}, s32[]{:T(128)}, bf16[1024,12,64]{0,2,1:T(8,128)(2,1)}, ...), branch_computations={%region_2.2_spmd, %region_3.5_spmd} | conditional | flops 263786112 | bytes 32158062 | solution.py:144
  158.9 4.0 fusion
  162.9 3.5 copy.117
  166.4 2.0 fusion.148
  169.8 2.5 fusion.8
  173.5 1.8 multiply_reduce_fusion.4
  179.7 54.7 %all_to_all.10 = bf16[8,8,8,1536]{3,2,1,0:T(8,128)(2,1)S(1)} all-to-all(bf16[8,8,8,1536]{3,2,1,0:T(8,128)(2,1)S(1)} %bitcast.243), channel_id=1, replica_groups=mesh['ctx'=8,'fsdp'=4] {'ctx'}, dimensions={0} | all-to-all | bytes 3145728 | tf_op jit(solution)/shard_map/all_to_all | solution.py:182
  236.0 45.2 %all-gather.7.cloned.1.call-done = bf16[4,8,64,1536]{3,2,1,0:T(8,128)(2,1)} async-done(((bf16[1,8,64,1536]{3,2,1,0:T(8,128)(2,1)}), bf16[4,8,64,1536]{3,2,1,0:T(8,128)(2,1)}) %all-gather.7.cloned.1.call-update) | async-done | bytes 6291472 | tf_op jit(solution)/shard_map/all_gather | solution.py:185
  281.2 3.2 copy.141
  284.4 7.4 %fusion.92 = f32[8,256,768]{2,1,0:T(8,128)S(1)} fusion(bf16[8,768,768]{2,1,0:T(8,128)(2,1)} %param.26, bf16[8,256,1536]{2,1,0:T(8,128)(2,1)S(1)} %bitcast.203), kind=kOutput, calls=%fused_computation.110 | convolution fusion | flops 2415919104 | bytes 18874368 | tf_op jit(solution)/shard_map/jcd,jdf->jcf/dot_general | solution.py:189
  291.8 9.6 %fusion.83 = bf16[8,256,768]{2,1,0:T(8,128)(2,1)S(1)} fusion(f32[8,256,768]{2,1,0:T(8,128)S(1)} %fusion.92, bf16[8,768,768]{2,1,0:T(8,128)(2,1)} %param.27, bf16[8,256,1536]{2,1,0:T(8,128)(2,1)S(1)} %bitcast.204), kind=kOutput, calls=%fused_computation.99 | convolution fusion | flops 2445803520 | bytes 22020096 | tf_op jit(solution)/shard_map/jcd,jfd->jcf/dot_general | solution.py:192
  301.4 9.8 %convolution_convert_fusion.2 = bf16[8,256,768]{2,1,0:T(8,128)(2,1)} fusion(bf16[8,768,768]{2,1,0:T(8,128)(2,1)} %param.27, f32[8,256,768]{2,1,0:T(8,128)S(1)} %fusion.92), kind=kOutput, calls=%fused_computation.113 | convolution fusion | flops 2431647744 | bytes 18874368 | tf_op jit(solution)/shard_map/jcf,jfd->jcd/dot_general | solution.py:194
  311.3 11.1 %convolution_convert_fusion.1 = bf16[8,256,768]{2,1,0:T(8,128)(2,1)} fusion(bf16[8,256,768]{2,1,0:T(8,128)(2,1)S(1)} %fusion.83, bf16[8,768,768]{2,1,0:T(8,128)(2,1)} %param.26), kind=kOutput, calls=%fused_computation.112 | convolution fusion | flops 2417491968 | bytes 15728640 | tf_op jit(solution)/shard_map/jcf,jdf->jcd/dot_general | solution.py:195
  322.4 3.3 pad_maximum_fusion.2
  325.7 3.4 copy.142
  329.1 59.0 %reduce-scatter.6.cloned.1.call-done = bf16[512,1536]{1,0:T(8,128)(2,1)} async-done(((bf16[2048,1536]{1,0:T(8,128)(2,1)}), bf16[512,1536]{1,0:T(8,128)(2,1)}) %reduce-scatter.6.cloned.1.call-update) | async-done | bytes 1572880 | tf_op jit(solution)/shard_map/reduce_scatter | solution.py:201
  388.1 2.7 copy.143
  390.8 5.5 all-to-all-start.1
  398.7 34.6 %all-to-all-done.1 = bf16[8,8,8,1536]{3,2,1,0:T(8,128)(2,1)S(1)} async-done(((bf16[8,8,8,1536]{3,2,1,0:T(8,128)(2,1)}), bf16[8,8,8,1536]{3,2,1,0:T(8,128)(2,1)S(1)}, u32[]{:S(2)}, u32[]{:S(2)}) %all-to-all-start.1) | async-done | bytes 1572896 | tf_op jit(solution)/shard_map/all_to_all | solution.py:205
  438.1 2.0 multiply_reduce_fusion.2
  442.3 2.1 copy.146
  445.5 1.6 reduce_sum.158
  450.6 17.5 %while.37 = (s32[]{:T(128)}, f32[128,12,64]{0,2,1:T(8,128)}, bf16[1024,12,64]{0,2,1:T(8,128)(2,1)}, bf16[1024,12,64]{0,2,1:T(8,128)(2,1)}, f32[12,32]{1,0:T(8,12...) while((s32[]{:T(128)}, f32[128,12,64]{0,2,1:T(8,128)}, ...), condition=%wide.region_25.26_spmd, body=%wide.region_22.25_spmd.sunk | while | flops 871040000 | bytes 62574376 | solution.py:281
  450.9 17.3 %conditional.5 = ((f32[128,12,64]{0,2,1:T(8,128)}, bf16[1024,12,64]{0,2,1:T(8,128)(2,1)}, bf16[1024,12,64]{0,2,1:T(8,128)(2,1)}, f32[12,32]{1,0:T(8,128)S(1)})) conditional(s32[]{:T(128)} %convert_element_type.574, (f32[128,12,64]{0,2,1:T(8,128)}, bf16[1024,12,64]{0,2,1:T(8,128)(2,1)}, bf16[1024,12,64]{0,2,1:T(8,128)(2,1)}, ...), branch_computations={%region_23.23_spmd, %region_24.24_spmd} | conditional | flops 871040000 | bytes 62574064 | solution.py:273
  451.6 2.0 fusion.33
  453.6 1.7 fusion.39
  458.6 2.1 fusion.45
  460.8 5.5 fusion.49
  468.2 2.2 pad_maximum_fusion.3
  470.4 2.9 copy.159
  474.3 2.0 fusion.151
  476.3 1.8 reshape.640
  481.2 2.9 fusion.143
  484.1 1.9 fusion.121
  486.0 77.2 %reduce-scatter.10.cloned.1.call-done = bf16[128,1536]{1,0:T(8,128)(2,1)} async-done(((bf16[1024,1536]{1,0:T(8,128)(2,1)}), bf16[128,1536]{1,0:T(8,128)(2,1)}) %reduce-scatter.10.cloned.1.call-update) | async-done | bytes 393232
  563.1 1.6 convolution_add_fusion.1
  564.8 2.3 fusion.113
  571.2 3.2 pad_maximum_fusion.1
  574.4 7.6 %pad_maximum_fusion = f32[32,104,768]{2,1,0:T(8,128)} fusion(f32[32,8,768]{2,1,0:T(8,128)S(1)} %bitcast.231, f32[32,24,768]{2,1,0:T(8,128)S(1)} %copy-done.9, f32[32,72,768]{2,1,0:T(8,128)} %bitcast.211), kind=kLoop, calls=%fused_computation.89 | loop fusion | flops 5111808 | bytes 20447232 | tf_op jit(solution)/shard_map/concatenate | solution.py:323
  582.0 13.0 %fusion.90 = f32[8,768,768]{2,1,0:T(8,128)} fusion(bf16[8,256,768]{2,1,0:T(8,128)(2,1)} %copy-done.8, bf16[8,256,1536]{2,1,0:T(8,128)(2,1)} %bitcast.205), kind=kOutput, calls=%fused_computation.108 | convolution fusion | flops 2415919104 | bytes 25165824 | tf_op jit(solution)/shard_map/jcd,jcf->jdf/dot_general | solution.py:203
  595.0 13.5 %fusion.84 = f32[8,768,768]{2,1,0:T(8,128)} fusion(bf16[8,256,1536]{2,1,0:T(8,128)(2,1)S(1)} %bitcast.208, f32[8,256,768]{2,1,0:T(8,128)} %copy-done.2), kind=kOutput, calls=%fused_computation.104 | convolution fusion | flops 2430074880 | bytes 28311552 | tf_op jit(solution)/shard_map/jcf,jcd->jfd/dot_general | solution.py:202
  609.5 111.7 %reduce-scatter.8.cloned.1.call-done = f32[1,104,768]{2,1,0:T(8,128)} async-done(((f32[32,104,768]{2,1,0:T(8,128)}), f32[1,104,768]{2,1,0:T(8,128)}) %reduce-scatter.8.cloned.1.call-update) | async-done | bytes 319504 | tf_op jit(solution)/shard_map/reduce_scatter | solution.py:331
  724.6 1.5 slice_bitcast_fusion.10
  726.1 1.6 slice_bitcast_fusion.9
  (228 shorter events, 73.1 us)
Async XLA Ops:
  7.2 71.8 %all-gather.9.cloned.1.call-start = ((), (), s32[]{:S(2)}) async-start(), calls=%async_computation.9 | async-start | bytes 5271552 | tf_op jit(solution)/shard_map/all_gather | solution.py:92
  11.2 140.2 %all-gather.5.cloned.1.call-start = ((), (), s32[]{:S(2)}) async-start(), calls=%async_computation.5 | async-start | bytes 3538944 | tf_op jit(solution)/shard_map/all_gather | solution.py:115
  83.0 45.0 %copy-start.6 = (bf16[32,72,768]{2,1,0:T(8,128)(2,1)}, bf16[32,72,768]{2,1,0:T(8,128)(2,1)S(1)}, u32[]{:S(2)}) copy-start(bf16[32,72,768]{2,1,0:T(8,128)(2,1)S(1)} %slice.131) | copy-start | bytes 10616836
  89.2 38.8 %copy-start.38 = (f32[768]{0:T(1024)}, f32[768]{0:T(1024)S(1)}, u32[]{:S(2)}) copy-start(f32[768]{0:T(1024)S(1)} %reshape.647) | copy-start | bytes 9220
  92.6 188.5 %all-gather.7.cloned.1.call-start = ((), (), s32[]{:S(2)}) async-start(), calls=%async_computation.6 | async-start | bytes 7864320 | tf_op jit(solution)/shard_map/all_gather | solution.py:185
  107.0 0.8 copy-start.22
  112.5 0.6 copy-start.44
  157.5 16.0 %copy-start.11 = (bf16[1,128,768]{2,1,0:T(8,128)(2,1)S(1)}, bf16[1,128,768]{2,1,0:T(8,128)(2,1)}, u32[]{:S(2)}) copy-start(bf16[1,128,768]{2,1,0:T(8,128)(2,1)} %param.18) | copy-start | bytes 589828
  168.4 1.4 copy-start.3
  172.3 4.5 copy-start.28
  172.3 4.8 copy-start.47
  172.3 6.5 copy-start.26
  172.4 6.6 copy-start.52
  173.5 3.4 copy-start.23
  175.3 0.8 copy-start.20
  175.3 0.7 copy-start.50
  176.9 57.6 %copy-start.27 = (bf16[128,768]{1,0:T(8,128)(2,1)}, bf16[128,768]{1,0:T(8,128)(2,1)S(1)}, u32[]{:S(2)}) copy-start(bf16[128,768]{1,0:T(8,128)(2,1)S(1)} %multiply_convert_fusion.2) | copy-start | bytes 589828
  177.2 0.6 copy-start.41
  177.2 0.6 copy-start.43
  177.8 0.5 copy-start.49
  178.2 56.2 %copy-start.46 = (f32[128,2]{0,1:T(2,128)}, f32[128,2]{0,1:T(2,128)S(1)}, u32[]{:S(2)}) copy-start(f32[128,2]{0,1:T(2,128)S(1)} %fusion.140) | copy-start | bytes 3076
  235.7 152.4 %reduce-scatter.6.cloned.1.call-start = ((), (), s32[]{:S(2)}) async-start(), calls=%async_computation.7 | async-start | bytes 7864320 | tf_op jit(solution)/shard_map/reduce_scatter | solution.py:201
  284.3 7.5 %copy-start.1 = (bf16[8,4,64,1536]{3,2,1,0:T(8,128)(2,1)}, bf16[8,4,64,1536]{3,2,1,0:T(8,128)(2,1)S(1)}, u32[]{:S(2)}) copy-start(bf16[8,4,64,1536]{3,2,1,0:T(8,128)(2,1)S(1)} %copy.141) | copy-start | bytes 18874372
  291.8 9.6 %copy-start.2 = (f32[8,256,768]{2,1,0:T(8,128)}, f32[8,256,768]{2,1,0:T(8,128)S(1)}, u32[]{:S(2)}) copy-start(f32[8,256,768]{2,1,0:T(8,128)S(1)} %fusion.92) | copy-start | bytes 18874372
  301.4 9.8 %copy-start.8 = (bf16[8,256,768]{2,1,0:T(8,128)(2,1)}, bf16[8,256,768]{2,1,0:T(8,128)(2,1)S(1)}, u32[]{:S(2)}) copy-start(bf16[8,256,768]{2,1,0:T(8,128)(2,1)S(1)} %fusion.83) | copy-start | bytes 9437188
  388.1 8.3 %copy-start.45 = (s32[256]{0:T(256)S(1)}, s32[256]{0:T(256)}, u32[]{:S(2)}) copy-start(s32[256]{0:T(256)} %copy-done.44) | copy-start | bytes 3076
  388.1 8.5 %copy-start.30 = (s32[1,128,2]{2,1,0:T(8,128)S(1)}, s32[1,128,2]{2,1,0:T(8,128)}, u32[]{:S(2)}) copy-start(s32[1,128,2]{2,1,0:T(8,128)} %copy.130) | copy-start | bytes 3076
  388.1 9.1 %copy-start.24 = (bf16[12,128,64]{1,2,0:T(8,128)(2,1)S(1)}, bf16[12,128,64]{1,2,0:T(8,128)(2,1)}, u32[]{:S(2)}) copy-start(bf16[12,128,64]{1,2,0:T(8,128)(2,1)} %copy-done.23) | copy-start | bytes 589828
  390.8 42.4 %all-to-all-start.1 = ((bf16[8,8,8,1536]{3,2,1,0:T(8,128)(2,1)}), bf16[8,8,8,1536]{3,2,1,0:T(8,128)(2,1)S(1)}, u32[]{:S(2)}, u32[]{:S(2)}) async-start(bf16[8,8,8,1536]{3,2,1,0:T(8,128)(2,1)} %copy.143), calls=%async_computation.2 | async-start | bytes 3145728 | tf_op jit(solution)/shard_map/all_to_all | solution.py:205
  396.4 166.8 %reduce-scatter.10.cloned.1.call-start = ((), (), s32[]{:S(2)}) async-start(), calls=%async_computation.10 | async-start | bytes 3538944
  397.2 40.9 %copy-start.29 = (bf16[768,64]{1,0:T(8,128)(2,1)S(1)}, bf16[768,64]{1,0:T(8,128)(2,1)}, u32[]{:S(2)}) copy-start(bf16[768,64]{1,0:T(8,128)(2,1)} %reshape.626) | copy-start | bytes 294916
  433.2 6.9 copy-start.21
  433.2 6.9 copy-start.33
  433.2 6.9 copy-start.40
  433.2 6.9 copy-start.51
  434.6 6.3 copy-start.5
  434.6 6.3 copy-start.32
  438.1 4.2 copy-start.37
  440.9 1.4 copy-start.17
  442.3 8.4 %copy-start = (bf16[1024,12,64]{0,2,1:T(8,128)(2,1)S(1)}, bf16[1024,12,64]{0,2,1:T(8,128)(2,1)}, u32[]{:S(2)}) copy-start(bf16[1024,12,64]{0,2,1:T(8,128)(2,1)} %get-tuple-element.881) | copy-start | bytes 4718596
  442.3 8.4 %copy-start.4 = (bf16[1024,12,64]{0,2,1:T(8,128)(2,1)S(1)}, bf16[1024,12,64]{0,2,1:T(8,128)(2,1)}, u32[]{:S(2)}) copy-start(bf16[1024,12,64]{0,2,1:T(8,128)(2,1)} %get-tuple-element.882) | copy-start | bytes 4718596
  442.3 8.4 %copy-start.35 = (f32[12,128]{1,0:T(8,128)S(1)}, f32[12,128]{1,0:T(8,128)}, u32[]{:S(2)}) copy-start(f32[12,128]{1,0:T(8,128)} %log_add_fusion) | copy-start | bytes 18436
  453.6 1.8 copy-start.36
  455.4 1.4 copy-start.13
  457.5 1.2 copy-start.14
  460.8 5.6 copy-start.15
  467.0 1.1 copy-start.16
  470.4 3.3 copy-start.42
  473.3 6.6 copy-start.7
  473.3 7.9 %copy-start.39 = (f32[768]{0:T(1024)S(1)}, f32[768]{0:T(1024)}, u32[]{:S(2)}) copy-start(f32[768]{0:T(1024)} %copy-done.38) | copy-start | bytes 9220
  473.3 247.8 %reduce-scatter.8.cloned.1.call-start = ((), (), s32[]{:S(2)}) async-start(), calls=%async_computation.8 | async-start | bytes 10543104 | tf_op jit(solution)/shard_map/reduce_scatter | solution.py:331
  474.3 6.9 copy-start.48
  478.8 5.3 copy-start.18
  478.8 5.3 copy-start.25
  567.1 2.4 copy-start.12
  567.1 2.4 copy-start.31
  569.5 1.7 copy-start.10
  571.2 3.2 copy-start.9
  582.0 13.0 %slice-start = ((s8[6291456]{0:T(1024)(128)(4,1)}), s8[2097152]{0:T(1024)(128)(4,1)S(1)}, s32[]{:S(2)}) async-start(s8[6291456]{0:T(1024)(128)(4,1)} %bitcast.206), calls=%async_computation.11 | async-start | bytes 4194304
  582.0 13.0 %slice-start.1 = ((s8[6291456]{0:T(1024)(128)(4,1)}), s8[4194304]{0:T(1024)(128)(4,1)S(1)}, s32[]{:S(2)}) async-start(s8[6291456]{0:T(1024)(128)(4,1)} %bitcast.206), calls=%async_computation.12 | async-start | bytes 8388608
  595.0 13.6 %copy-start.19 = (f32[128,768]{1,0:T(8,128)S(1)}, f32[128,768]{1,0:T(8,128)}, u32[]{:S(2)}) copy-start(f32[128,768]{1,0:T(8,128)} %copy-done.17) | copy-start | bytes 1179652
  595.0 13.6 %copy-start.34 = (f32[128,768]{1,0:T(8,128)S(1)}, f32[128,768]{1,0:T(8,128)}, u32[]{:S(2)}) copy-start(f32[128,768]{1,0:T(8,128)} %get-tuple-element.614) | copy-start | bytes 1179652
Sparse Core Ops, SparseCore 0:
  11.5 67.5 all-gather.8
  92.8 58.5 all-gather.4
  235.9 45.2 all-gather.6
  329.2 58.8 reduce-scatter.5
  473.4 89.6 reduce-scatter.9
  582.1 139.0 reduce-scatter.7
